TPU v7x, 32 devices: a whole 2x2x4 slice. The times are simulated.
32 devices in a mesh: grid: 8 (over y, x, core), sub: 4 (over z).
Axes of the slice: x: 2, y: 2, z: 4, core: 2. Of those that a mesh axis runs over, the one named last changes fastest.
Arguments:
- grid_x: bfloat16 [65536, 512], P(('grid', 'sub')), may hold values from -6 to 6
- mesh_h: bfloat16 [2048, 512], P(('grid', 'sub')), may hold values from -6 to 6
- gain_grid: float32 [512], replicated, may hold values from 0.1 to 1.9
- gain_mesh: float32 [512], replicated, may hold values from 0.1 to 1.9
- w_query: bfloat16 [512, 512], replicated, may hold values from -0.25 to 0.25
- w_key: bfloat16 [512, 512], replicated, may hold values from -0.25 to 0.25
- w_value: bfloat16 [512, 512], replicated, may hold values from -0.25 to 0.25
- w_out: bfloat16 [512, 512], replicated, may hold values from -0.25 to 0.25
- edge_bias: float32 [2048, 384], P(('grid', 'sub')), may hold values from -9 to 300
- neighbours: int32 [2048, 96], P(('grid', 'sub')), may hold values from 0 to 767, as said below
- valid: int32 [2048, 96], P(('grid', 'sub')), may hold values from 0 to 1, as said below
- send_rows: int32 [32, 3, 4, 64], P(('grid', 'sub')), may hold values from 0 to 2047, as said below
- out_grad: bfloat16 [2048, 512], P(('grid', 'sub')), may hold values from -24 to 24
Outputs:
- mesh_out: bfloat16 [2048, 512], P(('grid', 'sub'))
- mesh_grad: bfloat16 [2048, 512], P(('grid', 'sub'))
- grid_grad: bfloat16 [65536, 512], P(('grid', 'sub'))
- weight_grads: float32 [4, 512, 512], replicated
Inputs may be any that keep to these rules, and one draw needn't show every extreme that they name: `send_rows`: for each source device, slab offset and destination sub index the 64 local rows are distinct; rows sent to the slab below (o = 0) lie in the lower half of the device's 2048 rows, rows sent to the slab above (o = 2) in the upper half. `neighbours`: a slot (o * 4 + s) * 64 + t names row t of what device s of slab g - o + 1 sends to the node's device; slots of slabs outside the grid are never named; the 96 entries of a node are distinct; some slots are named by no node. The first two edges of every node are valid.
All inputs are finite; a program needn't handle non-finite values.
Results may differ from a plain program's by a relative error of at most 0.009.
Values may be sent and summed in bfloat16 or wider, within the bound.
A program may use at most 128 MiB of HBM per device.

v0:
```python
import jax
import jax.numpy as jnp
from jax import lax
from jax.sharding import PartitionSpec as P

EPSILON = 1e-06
NEG_FILL = -1e30


def from_behind(block, axis, distance):
    devices = range(lax.axis_size(axis))
    route = [(i - distance, i) for i in devices if i - distance in devices]
    return lax.ppermute(block, axis, route)


def normalize(values_in, gain_row):
    widened = values_in.astype(jnp.float32)
    factor = lax.rsqrt(jnp.mean(widened * widened, axis=-1, keepdims=True) + EPSILON)
    return (widened, factor, (widened * factor * gain_row).astype(jnp.bfloat16))


def normalize_back(widened, factor, gain_row, upstream):
    scaled = gain_row * upstream
    inner_mean = jnp.mean(widened * scaled, axis=-1, keepdims=True)
    return factor * scaled - widened * factor**3 * inner_mean


def shards(
    grid_x,
    mesh_h,
    gain_grid,
    gain_mesh,
    w_query,
    w_key,
    w_value,
    w_out,
    edge_bias,
    neighbours,
    valid,
    send_rows,
    out_grad,
):
    point_count, model_width = grid_x.shape
    node_count = mesh_h.shape[0]
    sub_count = send_rows.shape[2]
    slots_per = send_rows.shape[3]
    block = sub_count * slots_per
    slot_count = 3 * block
    fanout = neighbours.shape[1]
    head_count = edge_bias.shape[1] // fanout
    head_width = model_width // head_count
    logit_scale = head_width ** (-0.5)
    w_pair = jnp.concatenate([w_key, w_value], axis=1)
    grid_wide, grid_factor, grid_normed = normalize(grid_x, gain_grid)
    flat_rows = send_rows[0].reshape(slot_count)
    send_match = flat_rows[:, None] == jnp.arange(point_count, dtype=jnp.int32)[None, :]
    send_onehot = send_match.astype(jnp.bfloat16)
    sent_normed = jnp.dot(send_onehot, grid_normed, preferred_element_type=jnp.float32).astype(
        jnp.bfloat16
    )
    packet = sent_normed.reshape(3, sub_count, slots_per, model_width)
    packet_width = packet.shape[3]
    mixed = lax.all_to_all(packet, "sub", split_axis=1, concat_axis=1, tiled=True).reshape(
        3, block, packet_width
    )
    pieces = []
    for offset in (0, 1, 2):
        piece = mixed[offset]
        if offset != 1:
            piece = from_behind(piece, "grid", offset - 1)
        pieces.append(piece)
    arrived = jnp.concatenate(pieces, axis=0)
    recv_pair = jnp.dot(arrived, w_pair, preferred_element_type=jnp.float32).astype(jnp.bfloat16)
    slot_onehot = (
        neighbours[:, :, None] == jnp.arange(slot_count, dtype=jnp.int32)[None, None, :]
    ).astype(jnp.bfloat16)
    edge_pair = jnp.einsum(
        "gjc,ce->gje", slot_onehot, recv_pair, preferred_element_type=jnp.float32
    ).astype(jnp.bfloat16)
    edge_keys = edge_pair[:, :, :model_width].reshape(node_count, fanout, head_count, head_width)
    edge_values = edge_pair[:, :, model_width:].reshape(node_count, fanout, head_count, head_width)
    mesh_wide, mesh_factor, mesh_normed = normalize(mesh_h, gain_mesh)
    queries = (
        jnp.dot(mesh_normed, w_query, preferred_element_type=jnp.float32) * logit_scale
    ).astype(jnp.bfloat16)
    query_head_rows = queries.reshape(node_count, head_count, head_width)
    score_matrix = jnp.einsum(
        "gip,gjip->gij", query_head_rows, edge_keys, preferred_element_type=jnp.float32
    ) + edge_bias.reshape(node_count, head_count, fanout)
    live_mask = (valid == 1)[:, None, :]
    row_peak = jnp.max(jnp.where(live_mask, score_matrix, NEG_FILL), axis=2, keepdims=True)
    exp_terms = jnp.exp(jnp.where(live_mask, score_matrix - row_peak, NEG_FILL))
    attn_probs = exp_terms / jnp.sum(exp_terms, axis=2, keepdims=True)
    probabilities_batch = attn_probs.astype(jnp.bfloat16)
    attended_rows = (
        jnp.einsum(
            "gij,gjik->gik", probabilities_batch, edge_values, preferred_element_type=jnp.float32
        )
        .reshape(node_count, model_width)
        .astype(jnp.bfloat16)
    )
    mesh_out = (
        mesh_wide + jnp.dot(attended_rows, w_out, preferred_element_type=jnp.float32)
    ).astype(jnp.bfloat16)
    grad_wo = jnp.einsum("md,me->de", attended_rows, out_grad, preferred_element_type=jnp.float32)
    att_grad = jnp.einsum("me,de->md", out_grad, w_out, preferred_element_type=jnp.float32).astype(
        jnp.bfloat16
    )
    head_gradient = att_grad.reshape(node_count, head_count, head_width)
    probability_gradient = jnp.einsum(
        "gip,gjip->gij", head_gradient, edge_values, preferred_element_type=jnp.float32
    )
    score_gradient = (
        attn_probs
        * (probability_gradient - jnp.sum(attn_probs * probability_gradient, axis=2, keepdims=True))
    ).astype(jnp.bfloat16)
    query_gradient = (
        (
            jnp.einsum(
                "gij,gjik->gik", score_gradient, edge_keys, preferred_element_type=jnp.float32
            )
            * logit_scale
        )
        .reshape(node_count, model_width)
        .astype(jnp.bfloat16)
    )
    dense_score_gradient = jnp.einsum(
        "gij,gjc->gic", score_gradient, slot_onehot, preferred_element_type=jnp.float32
    ).astype(jnp.bfloat16)
    dense_probabilities = jnp.einsum(
        "gij,gjc->gic", probabilities_batch, slot_onehot, preferred_element_type=jnp.float32
    ).astype(jnp.bfloat16)
    key_part = jnp.einsum(
        "uza,uzt->azt", dense_score_gradient, query_head_rows, preferred_element_type=jnp.float32
    ).reshape(slot_count, model_width)
    value_part = jnp.einsum(
        "uza,uzt->azt", dense_probabilities, head_gradient, preferred_element_type=jnp.float32
    ).reshape(slot_count, model_width)
    back_packet = (
        jnp.concatenate([key_part, value_part], axis=1)
        .astype(jnp.bfloat16)
        .reshape(3, block, 2 * model_width)
    )
    home_pieces = []
    for offset in (0, 1, 2):
        piece = back_packet[offset]
        if offset != 1:
            piece = from_behind(piece, "grid", 1 - offset)
        home_pieces.append(piece)
    home = jnp.stack(home_pieces)
    home = home.reshape(3, sub_count, slots_per, 2 * model_width)
    returned = lax.all_to_all(home, "sub", split_axis=1, concat_axis=1, tiled=True).reshape(
        slot_count, 2 * model_width
    )
    pair_grads = jnp.einsum("sd,se->de", sent_normed, returned, preferred_element_type=jnp.float32)
    slot_back = jnp.einsum("se,de->sd", returned, w_pair, preferred_element_type=jnp.float32)
    normed_grad = jnp.einsum(
        "sp,sd->pd",
        send_match.astype(jnp.float32),
        slot_back,
        precision=lax.Precision.HIGHEST,
        preferred_element_type=jnp.float32,
    )
    grid_grad = normalize_back(grid_wide, grid_factor, gain_grid, normed_grad).astype(jnp.bfloat16)
    grad_wq = jnp.einsum(
        "md,me->de", mesh_normed, query_gradient, preferred_element_type=jnp.float32
    )
    mesh_normed_grad = jnp.einsum(
        "me,de->md", query_gradient, w_query, preferred_element_type=jnp.float32
    )
    mesh_grad = (
        out_grad.astype(jnp.float32)
        + normalize_back(mesh_wide, mesh_factor, gain_mesh, mesh_normed_grad)
    ).astype(jnp.bfloat16)
    local_grads = jnp.stack(
        [grad_wq, pair_grads[:, :model_width], pair_grads[:, model_width:], grad_wo]
    )
    weight_grads = lax.psum(local_grads, ("grid", "sub"))
    return (mesh_out, mesh_grad, grid_grad, weight_grads)


def solution(mesh):
    in_specs = (
        P(("grid", "sub"), None),
        P(("grid", "sub"), None),
        P(),
        P(),
        P(),
        P(),
        P(),
        P(),
        P(("grid", "sub"), None),
        P(("grid", "sub"), None),
        P(("grid", "sub"), None),
        P(("grid", "sub"), None, None, None),
        P(("grid", "sub"), None),
    )
    out_specs = (P(("grid", "sub"), None), P(("grid", "sub"), None), P(("grid", "sub"), None), P())
    return jax.shard_map(shards, mesh=mesh, in_specs=in_specs, out_specs=out_specs, check_vma=False)
```

profile of v0, /device:TPU:0, one launch (start us, length us, event | category | flops | bytes accessed | tf_op | source)
XLA Modules:
  0.0 303.4 jit_solution(8482572767754308976)
XLA Ops:
  7.2 3.0 copy.27
  10.8 2.0 fusion.35
  14.6 6.3 %all-to-all-start = ((bf16[3,4,64,512]{3,2,0,1:T(8,128)(2,1)}), bf16[3,4,64,512]{3,2,0,1:T(8,128)(2,1)S(1)}, u32[]{:S(2)}, u32[]{:S(2)}) async-start(bf16[3,4,64,512]{3,2,0,1:T(8,128)(2,1)} %copy.28), calls=%async_computation | async-start | bytes 1572864 | tf_op jit(solution)/shard_map/all_to_all | solution.py:63
  21.1 1.9 constant_dynamic-update-slice_fusion.1
  24.1 17.0 %all-to-all-done = bf16[3,4,64,512]{3,2,0,1:T(8,128)(2,1)S(1)} async-done(((bf16[3,4,64,512]{3,2,0,1:T(8,128)(2,1)}), bf16[3,4,64,512]{3,2,0,1:T(8,128)(2,1)S(1)}, u32[]{:S(2)}, u32[]{:S(2)}) %all-to-all-start) | async-done | bytes 786464 | tf_op jit(solution)/shard_map/all_to_all | solution.py:63
  41.1 1.3 collective-permute-start
  42.4 3.2 %collective-permute-start.1 = (bf16[256,512]{1,0:T(8,128)(2,1)S(1)}, bf16[256,512]{1,0:T(8,128)(2,1)S(1)}, u32[]{:S(2)}, u32[]{:S(2)}) collective-permute-start(bf16[256,512]{1,0:T(8,128)(2,1)S(1)} %bitcast.119), channel_id=1, source_target_pairs={{0,4},{4,8},{8,12},{12,16},{16,20},{20,24},{24,28},{1,5},{5,9},{9,... | collective-permute-start | bytes 786440 | tf_op jit(solution)/shard_map/ppermute | solution.py:13
  46.8 2.2 fusion.123
  49.0 11.4 %fusion.7 = bf16[64,96,1024]{2,1,0:T(8,128)(2,1)S(1)} fusion(s32[64,96]{1,0:T(8,128)} %param.22, bf16[768,1024,1]{1,0,2:T(8,128)(2,1)S(1)} %fusion.123), kind=kOutput, calls=%fused_computation.12 | convolution fusion | flops 9674686464 | bytes 14180352 | tf_op jit(solution)/shard_map/gjc,ce->gje/dot_general | solution.py:77
  60.5 3.7 %slice_bitcast_fusion.1 = (bf16[64,12,4,8,128]{4,3,2,1,0:T(8,128)(2,1)S(1)}, bf16[64,12,4,8,128]{4,3,2,1,0:T(8,128)(2,1)S(1)}) fusion(bf16[64,96,1024]{2,1,0:T(8,128)(2,1)S(1)} %fusion.7), kind=kLoop, calls=%fused_computation.22 | loop fusion | bytes 25165824
  64.2 3.3 %fusion.14 = f32[64,4,1,96]{3,2,1,0:T(1,128)S(1)} fusion(bf16[64,4,128,1]{2,3,1,0:T(2,128)(2,1)S(1)} %reshape.124, bf16[64,12,4,8,128]{4,3,2,1,0:T(8,128)(2,1)S(1)} %get-tuple-element.16), kind=kOutput, calls=%fused_computation.19 | convolution fusion | flops 6291456 | bytes 6455296 | tf_op jit(solution)/shard_map/gip,gjip->gij/dot_general | solution.py:87
  67.6 3.3 %fusion.8 = f32[64,4,1,96]{3,2,1,0:T(1,128)S(1)} fusion(bf16[64,4,128,1]{2,3,1,0:T(2,128)(2,1)S(1)} %reshape.126, bf16[64,12,4,8,128]{4,3,2,1,0:T(8,128)(2,1)S(1)} %get-tuple-element.17), kind=kOutput, calls=%fused_computation.13 | convolution fusion | flops 6291456 | bytes 6455296 | tf_op jit(solution)/shard_map/gip,gjip->gij/dot_general | solution.py:110
  71.2 3.6 %fusion.39 = bf16[64,4,768]{2,1,0:T(4,128)(2,1)S(1)} fusion(s32[64,96]{1,0:T(8,128)S(1)} %copy-done.29, f32[64,4,96]{2,1,0:T(4,128)S(1)} %get-tuple-element.33, f32[64,4]{1,0:T(8,128)S(1)} %get-tuple-element.32), kind=kOutput, calls=%fused_computation.55 | convolution fusion | flops 42713088 | bytes 517120 | tf_op jit(solution)/shard_map/gij,gjc->gic/dot_general | solution.py:130
  75.8 3.5 %fusion.38 = bf16[64,4,768]{2,1,0:T(4,128)(2,1)S(1)} fusion(bf16[64,4,96]{2,1,0:T(4,128)(2,1)S(1)} %get-tuple-element.26, s32[64,96]{1,0:T(8,128)S(1)} %copy-done.29), kind=kOutput, calls=%fused_computation.54 | convolution fusion | flops 42663936 | bytes 466944 | tf_op jit(solution)/shard_map/gij,gjc->gic/dot_general | solution.py:127
  81.0 5.0 %collective-permute-start.2 = (bf16[256,1024]{1,0:T(8,128)(2,1)S(1)}, bf16[256,1024]{1,0:T(8,128)(2,1)S(1)}, u32[]{:S(2)}, u32[]{:S(2)}) collective-permute-start(bf16[256,1024]{1,0:T(8,128)(2,1)S(1)} %get-tuple-element.20), channel_id=1, source_target_pairs={{0,4},{4,8},{8,12},{12,16},{16,20},{20,24},{24,28},{1,5},{5,9},{9,... | collective-permute-start | bytes 1572872 | tf_op jit(solution)/shard_map/ppermute | solution.py:13
  86.0 1.3 collective-permute-start.3
  87.5 4.3 %collective-permute-done.3 = bf16[256,1024]{1,0:T(8,128)(2,1)S(1)} collective-permute-done((bf16[256,1024]{1,0:T(8,128)(2,1)S(1)}, bf16[256,1024]{1,0:T(8,128)(2,1)S(1)}, u32[]{:S(2)}, u32[]{:S(2)}) %collective-permute-start.3) | collective-permute-done | bytes 524320 | tf_op jit(solution)/shard_map/ppermute | solution.py:13
  91.9 1.3 copy.35
  93.2 4.4 %all-to-all-start.1 = ((bf16[3,4,64,1024]{3,2,0,1:T(8,128)(2,1)}), bf16[3,4,64,1024]{3,2,0,1:T(8,128)(2,1)}, u32[]{:S(2)}, u32[]{:S(2)}) async-start(bf16[3,4,64,1024]{3,2,0,1:T(8,128)(2,1)} %copy.35), calls=%async_computation.1 | async-start | bytes 3145728 | tf_op jit(solution)/shard_map/all_to_all | solution.py:152
  97.9 4.7 %fusion.10 = f32[64,4,1,128]{3,2,1,0:T(1,128)S(1)} fusion(bf16[64,12,4,8,128]{4,3,2,1,0:T(8,128)(2,1)} %copy-done.2, bf16[64,4,96,1]{2,1,0,3:T(4,128)(2,1)S(1)} %copy-done.16), kind=kOutput, calls=%fused_computation.15 | convolution fusion | flops 6291456 | bytes 6471680 | tf_op jit(solution)/shard_map/gij,gjik->gik/dot_general | solution.py:96
  102.6 1.3 convolution_bitcast_fusion
  103.9 1.7 fusion.12
  106.5 24.3 %all-to-all-done.1 = bf16[3,4,64,1024]{3,2,0,1:T(8,128)(2,1)} async-done(((bf16[3,4,64,1024]{3,2,0,1:T(8,128)(2,1)}), bf16[3,4,64,1024]{3,2,0,1:T(8,128)(2,1)}, u32[]{:S(2)}, u32[]{:S(2)}) %all-to-all-start.1) | async-done | bytes 1572896 | tf_op jit(solution)/shard_map/all_to_all | solution.py:152
  130.8 1.6 copy.36
  132.4 1.0 fusion.94
  134.2 2.5 pad_maximum_fusion
  138.8 2.7 fusion.93
  141.6 6.1 %fusion.28 = (f32[2048]{0:T(1024)S(1)}, f32[2048,512]{0,1:T(8,128)S(1)}) fusion(bf16[2048,512]{0,1:T(8,128)(2,1)S(1)} %copy-done.4, f32[512]{0:T(512)S(1)} %copy-done.27, f32[768,512]{1,0:T(8,128)S(1)} %fusion.93, s32[768]{0:T(1024)S(1)} %copy-done.25), kind=kOutput, calls=%fused_computation.36 | convolution fusion | flops 9669441536 | bytes 7877632 | tf_op jit(solution)/shard_map/sp,sd->pd/dot_general | solution.py:157
  147.7 2.6 fusion.27
  150.3 3.9 %copy.37 = bf16[2048,512]{1,0:T(8,128)(2,1)} copy(bf16[2048,512]{0,1:T(8,128)(2,1)} %fusion.27) | data formatting | bytes 4194304
  154.2 137.7 %all-reduce.2.cloned.1.call-done = f32[4,512,512]{2,1,0:T(8,128)} async-done(((f32[4,512,512]{2,1,0:T(8,128)}), f32[4,512,512]{2,1,0:T(8,128)}) %all-reduce.2.cloned.1.call-update) | async-done | bytes 4194320 | tf_op jit(solution)/shard_map/psum | solution.py:178
  291.9 4.6 %copy.106 = f32[4,512,512]{2,1,0:T(8,128)} copy(f32[4,512,512]{2,1,0:T(8,128)} %all-reduce.2.cloned.1.call-done) | data formatting | bytes 8388608
  (102 shorter events, 12.1 us)
Async XLA Ops:
  7.2 16.6 %copy-start = (bf16[512,512]{1,0:T(8,128)(2,1)S(1)}, bf16[512,512]{1,0:T(8,128)(2,1)}, u32[]{:S(2)}) copy-start(bf16[512,512]{1,0:T(8,128)(2,1)} %param.17) | copy-start | bytes 1572868
  7.2 3.5 %copy-start.20 = (s32[1,3,4,64]{3,2,1,0:T(4,128)S(1)}, s32[1,3,4,64]{3,2,1,0:T(4,128)}, u32[]{:S(2)}) copy-start(s32[1,3,4,64]{3,2,1,0:T(4,128)} %param.24) | copy-start | bytes 9220
  7.2 3.6 %copy-start.26 = (f32[512]{0:T(512)S(1)}, f32[512]{0:T(512)}, u32[]{:S(2)}) copy-start(f32[512]{0:T(512)} %param.15) | copy-start | bytes 6148
  10.2 2.5 copy-start.3
  10.8 10.2 %copy-start.6 = (bf16[64,512]{1,0:T(8,128)(2,1)S(1)}, bf16[64,512]{1,0:T(8,128)(2,1)}, u32[]{:S(2)}) copy-start(bf16[64,512]{1,0:T(8,128)(2,1)} %param.14) | copy-start | bytes 196612
  12.8 10.7 %copy-start.7 = (bf16[512,512]{1,0:T(8,128)(2,1)S(1)}, bf16[512,512]{1,0:T(8,128)(2,1)}, u32[]{:S(2)}) copy-start(bf16[512,512]{1,0:T(8,128)(2,1)} %param.20) | copy-start | bytes 1572868
  12.8 10.7 %copy-start.11 = (bf16[64,512]{1,0:T(8,128)(2,1)S(1)}, bf16[64,512]{1,0:T(8,128)(2,1)}, u32[]{:S(2)}) copy-start(bf16[64,512]{1,0:T(8,128)(2,1)} %param.25) | copy-start | bytes 196612
  13.7 10.1 %copy-start.18 = (f32[512]{0:T(512)S(1)}, f32[512]{0:T(512)}, u32[]{:S(2)}) copy-start(f32[512]{0:T(512)} %param.16) | copy-start | bytes 6148
  13.7 32.0 %copy-start.12 = (bf16[512,512]{1,0:T(8,128)(2,1)S(1)}, bf16[512,512]{1,0:T(8,128)(2,1)}, u32[]{:S(2)}) copy-start(bf16[512,512]{1,0:T(8,128)(2,1)} %param.19) | copy-start | bytes 1572868
  13.7 32.9 %copy-start.13 = (f32[64,384]{1,0:T(8,128)S(1)}, f32[64,384]{1,0:T(8,128)}, u32[]{:S(2)}) copy-start(f32[64,384]{1,0:T(8,128)} %param.21) | copy-start | bytes 294916
  13.7 33.1 %copy-start.17 = (s32[64,96]{1,0:T(8,128)S(1)}, s32[64,96]{1,0:T(8,128)}, u32[]{:S(2)}) copy-start(s32[64,96]{1,0:T(8,128)} %param.23) | copy-start | bytes 73732
  14.6 26.5 %all-to-all-start = ((bf16[3,4,64,512]{3,2,0,1:T(8,128)(2,1)}), bf16[3,4,64,512]{3,2,0,1:T(8,128)(2,1)S(1)}, u32[]{:S(2)}, u32[]{:S(2)}) async-start(bf16[3,4,64,512]{3,2,0,1:T(8,128)(2,1)} %copy.28), calls=%async_computation | async-start | bytes 1572864 | tf_op jit(solution)/shard_map/all_to_all | solution.py:63
  41.1 5.7 %collective-permute-start = (bf16[256,512]{1,0:T(8,128)(2,1)S(1)}, bf16[256,512]{1,0:T(8,128)(2,1)S(1)}, u32[]{:S(2)}, u32[]{:S(2)}) collective-permute-start(bf16[256,512]{1,0:T(8,128)(2,1)S(1)} %bitcast.120), channel_id=1, source_target_pairs={{4,0},{8,4},{12,8},{16,12},{20,16},{24,20},{28,24},{5,1},{9,5},{13... | collective-permute-start | bytes 786440 | tf_op jit(solution)/shard_map/ppermute | solution.py:13
  42.4 4.4 %collective-permute-start.1 = (bf16[256,512]{1,0:T(8,128)(2,1)S(1)}, bf16[256,512]{1,0:T(8,128)(2,1)S(1)}, u32[]{:S(2)}, u32[]{:S(2)}) collective-permute-start(bf16[256,512]{1,0:T(8,128)(2,1)S(1)} %bitcast.119), channel_id=1, source_target_pairs={{0,4},{4,8},{8,12},{12,16},{16,20},{20,24},{24,28},{1,5},{5,9},{9,... | collective-permute-start | bytes 786440 | tf_op jit(solution)/shard_map/ppermute | solution.py:13
  64.2 6.7 %copy-start.1 = (bf16[64,12,4,8,128]{4,3,2,1,0:T(8,128)(2,1)}, bf16[64,12,4,8,128]{4,3,2,1,0:T(8,128)(2,1)S(1)}, u32[]{:S(2)}) copy-start(bf16[64,12,4,8,128]{4,3,2,1,0:T(8,128)(2,1)S(1)} %get-tuple-element.16) | copy-start | bytes 18874372
  64.2 6.7 %copy-start.2 = (bf16[64,12,4,8,128]{4,3,2,1,0:T(8,128)(2,1)}, bf16[64,12,4,8,128]{4,3,2,1,0:T(8,128)(2,1)S(1)}, u32[]{:S(2)}) copy-start(bf16[64,12,4,8,128]{4,3,2,1,0:T(8,128)(2,1)S(1)} %get-tuple-element.17) | copy-start | bytes 18874372
  67.6 3.6 %copy-start.29 = (s32[64,96]{1,0:T(8,128)S(1)}, s32[64,96]{1,0:T(8,128)}, u32[]{:S(2)}) copy-start(s32[64,96]{1,0:T(8,128)} %param.22) | copy-start | bytes 73732
  75.8 4.0 %copy-start.14 = (bf16[64,4,96]{2,1,0:T(4,128)(2,1)}, bf16[64,4,96]{2,1,0:T(4,128)(2,1)S(1)}, u32[]{:S(2)}) copy-start(bf16[64,4,96]{2,1,0:T(4,128)(2,1)S(1)} %get-tuple-element.26) | copy-start | bytes 147460
  81.0 6.5 %collective-permute-start.2 = (bf16[256,1024]{1,0:T(8,128)(2,1)S(1)}, bf16[256,1024]{1,0:T(8,128)(2,1)S(1)}, u32[]{:S(2)}, u32[]{:S(2)}) collective-permute-start(bf16[256,1024]{1,0:T(8,128)(2,1)S(1)} %get-tuple-element.20), channel_id=1, source_target_pairs={{0,4},{4,8},{8,12},{12,16},{16,20},{20,24},{24,28},{1,5},{5,9},{9,... | collective-permute-start | bytes 1572872 | tf_op jit(solution)/shard_map/ppermute | solution.py:13
  86.0 5.8 %collective-permute-start.3 = (bf16[256,1024]{1,0:T(8,128)(2,1)S(1)}, bf16[256,1024]{1,0:T(8,128)(2,1)S(1)}, u32[]{:S(2)}, u32[]{:S(2)}) collective-permute-start(bf16[256,1024]{1,0:T(8,128)(2,1)S(1)} %get-tuple-element.21), channel_id=1, source_target_pairs={{4,0},{8,4},{12,8},{16,12},{20,16},{24,20},{28,24},{5,1},{9,5},{13... | collective-permute-start | bytes 1572872 | tf_op jit(solution)/shard_map/ppermute | solution.py:13
  91.7 6.1 %copy-start.16 = (bf16[64,4,96,1]{2,1,0,3:T(4,128)(2,1)S(1)}, bf16[64,4,96,1]{2,1,0,3:T(4,128)(2,1)}, u32[]{:S(2)}) copy-start(bf16[64,4,96,1]{2,1,0,3:T(4,128)(2,1)} %get-tuple-element.27) | copy-start | bytes 147460
  91.9 12.0 %slice-start = ((s8[6291456]{0:T(1024)(128)(4,1)}), s8[2097152]{0:T(1024)(128)(4,1)S(1)}, s32[]{:S(2)}) async-start(s8[6291456]{0:T(1024)(128)(4,1)} %bitcast.102), calls=%async_computation.3 | async-start | bytes 4194304
  93.2 37.6 %all-to-all-start.1 = ((bf16[3,4,64,1024]{3,2,0,1:T(8,128)(2,1)}), bf16[3,4,64,1024]{3,2,0,1:T(8,128)(2,1)}, u32[]{:S(2)}, u32[]{:S(2)}) async-start(bf16[3,4,64,1024]{3,2,0,1:T(8,128)(2,1)} %copy.35), calls=%async_computation.1 | async-start | bytes 3145728 | tf_op jit(solution)/shard_map/all_to_all | solution.py:152
  97.6 194.4 %all-reduce.2.cloned.1.call-start = ((), (), s32[]{:S(2)}) async-start(), calls=%async_computation.2 | async-start | bytes 8388608 | tf_op jit(solution)/shard_map/psum | solution.py:178
  97.8 6.0 %copy-start.15 = (bf16[64,4,96]{2,1,0:T(4,128)(2,1)S(1)}, bf16[64,4,96]{2,1,0:T(4,128)(2,1)}, u32[]{:S(2)}) copy-start(bf16[64,4,96]{2,1,0:T(4,128)(2,1)} %copy-done.14) | copy-start | bytes 147460
  97.9 6.0 %slice-start.1 = ((s8[6291456]{0:T(1024)(128)(4,1)}), s8[4194304]{0:T(1024)(128)(4,1)S(1)}, s32[]{:S(2)}) async-start(s8[6291456]{0:T(1024)(128)(4,1)} %bitcast.102), calls=%async_computation.4 | async-start | bytes 8388608
  102.5 3.1 %copy-start.19 = (f32[512]{0:T(512)S(1)}, f32[512]{0:T(512)}, u32[]{:S(2)}) copy-start(f32[512]{0:T(512)} %param.16) | copy-start | bytes 6148
  102.5 3.1 %copy-start.22 = (f32[64]{0:T(128)S(1)}, f32[64]{0:T(128)}, u32[]{:S(2)}) copy-start(f32[64]{0:T(128)} %copy-done.21) | copy-start | bytes 772
  105.6 26.8 %copy-start.10 = (bf16[768,512]{1,0:T(8,128)(2,1)S(1)}, bf16[768,512]{1,0:T(8,128)(2,1)}, u32[]{:S(2)}) copy-start(bf16[768,512]{1,0:T(8,128)(2,1)} %copy-done.9) | copy-start | bytes 2359300
  136.6 4.9 %copy-start.4 = (bf16[2048,512]{0,1:T(8,128)(2,1)S(1)}, bf16[2048,512]{0,1:T(8,128)(2,1)}, u32[]{:S(2)}) copy-start(bf16[2048,512]{0,1:T(8,128)(2,1)} %copy-done.3) | copy-start | bytes 6291460
  136.6 4.9 %copy-start.25 = (s32[768]{0:T(1024)S(1)}, s32[768]{0:T(1024)}, u32[]{:S(2)}) copy-start(s32[768]{0:T(1024)} %copy-done.24) | copy-start | bytes 9220
  136.6 4.9 %copy-start.27 = (f32[512]{0:T(512)S(1)}, f32[512]{0:T(512)}, u32[]{:S(2)}) copy-start(f32[512]{0:T(512)} %param.15) | copy-start | bytes 6148
  (7 other events, 7.8 us)
Sparse Core Ops, SparseCore 0:
  136.8 155.1 all-reduce.1
where the time goes:
time: 304 us; the launch traced here: 303 us
  waiting for transfers between devices  184 us (61%)
  matrix products  49.8 us (16%)
  local copies, waits for them, and re-layouts  25.1 us (8%)
  starting transfers between devices  21.8 us (7%)
  between operations  14.6 us (5%)
  other arithmetic  8.64 us (3%)
    psum x1, waiting for transfers between devices, shards(): weight_grads = lax.psum(local_grads, ('grid', 'sub'))  138 us
    all_to_all x1, waiting for transfers between devices, shards(): lax.all_to_all(home, 'sub', split_axis=1, concat_axis=1, tiled=True)  24.3 us
    unnamed x69, local copies, waits for them, and re-layouts  19.4 us
    all_to_all x1, waiting for transfers between devices, shards(): lax.all_to_all(packet, 'sub', split_axis=1, concat_axis=1, tiled=True)  17 us
    dot_general x1, matrix products, shards(): jnp.einsum('gjc,ce->gje', slot_onehot, recv_pair, preferred_element_type=...  11.4 us
    ppermute x4, starting transfers between devices, from_behind(): return lax.ppermute(block, axis, route)  10.8 us
    all_to_all x1, starting transfers between devices, shards(): lax.all_to_all(packet, 'sub', split_axis=1, concat_axis=1, tiled=True)  6.35 us
    dot_general x1, matrix products, shards(): jnp.einsum('sp,sd->pd', send_match.astype(jnp.float32), slot_back, precis...  6.08 us
  transfers between devices with their start and end apart: 7, of which 5 were waited for; matrix products, arithmetic and copies ran while one was open for 10% of the time, Pallas kernels for 0%

commit v1 on v0

--- a/solution.py
+++ b/solution.py
@@ -175,7 +175,13 @@
     local_grads = jnp.stack(
         [grad_wq, pair_grads[:, :model_width], pair_grads[:, model_width:], grad_wo]
     )
-    weight_grads = lax.psum(local_grads, ("grid", "sub"))
+
+    def use_layers_all_here(x0, dev_axis, link_axis):
+        for d in (dev_axis, link_axis):
+            x0 = lax.psum(x0, axis_name=d)
+        return x0
+
+    weight_grads = use_layers_all_here(local_grads, "sub", link_axis="grid")
     return (mesh_out, mesh_grad, grid_grad, weight_grads)
 
 

time: 304 us -> 400 us (1.32)
  waiting for transfers between devices: 184 us -> 278 us
    psum x1 -> x2, waiting for transfers between devices: 138 us -> 232 us  [use_layers_all_here(): x0 = lax.psum(x0, axis_name=d)]
    unnamed x69 -> x67, local copies, waits for them, and re-layouts: 19.4 us -> 19.4 us
  transfers between devices with their start and end apart: 7 -> 8, of which waited for: 5 -> 5; matrix products, arithmetic and copies ran while one was open for 10% -> 8% of each run, Pallas kernels for 0% -> 0%
where the time goes in v1:
time: 400 us; the launch traced here: 399 us
  waiting for transfers between devices  278 us (70%)
  matrix products  49.8 us (12%)
  local copies, waits for them, and re-layouts  25.1 us (6%)
  starting transfers between devices  21.9 us (5%)
  between operations  14.6 us (4%)
  other arithmetic  9.3 us (2%)
    psum x2, waiting for transfers between devices, use_layers_all_here(): x0 = lax.psum(x0, axis_name=d)  232 us
    all_to_all x1, waiting for transfers between devices, shards(): lax.all_to_all(home, 'sub', split_axis=1, concat_axis=1, tiled=True)  25 us
    unnamed x67, local copies, waits for them, and re-layouts  19.4 us
    all_to_all x1, waiting for transfers between devices, shards(): lax.all_to_all(packet, 'sub', split_axis=1, concat_axis=1, tiled=True)  17 us
    dot_general x1, matrix products, shards(): jnp.einsum('gjc,ce->gje', slot_onehot, recv_pair, preferred_element_type=...  11.4 us
    ppermute x4, starting transfers between devices, from_behind(): return lax.ppermute(block, axis, route)  11 us
  transfers between devices with their start and end apart: 8, of which 5 were waited for; matrix products, arithmetic and copies ran while one was open for 8% of the time, Pallas kernels for 0%

profile of v1, /device:TPU:0, one launch (start us, length us, event | category | flops | bytes accessed | tf_op | source)
XLA Modules:
  0.0 399.0 jit_solution(14096659698154937789)
XLA Ops:
  7.2 3.0 copy.27
  10.8 2.0 fusion.35
  14.6 6.3 %all-to-all-start = ((bf16[3,4,64,512]{3,2,0,1:T(8,128)(2,1)}), bf16[3,4,64,512]{3,2,0,1:T(8,128)(2,1)S(1)}, u32[]{:S(2)}, u32[]{:S(2)}) async-start(bf16[3,4,64,512]{3,2,0,1:T(8,128)(2,1)} %copy.28), calls=%async_computation | async-start | bytes 1572864 | tf_op jit(solution)/shard_map/all_to_all | solution.py:63
  21.1 1.9 constant_dynamic-update-slice_fusion.1
  24.0 17.0 %all-to-all-done = bf16[3,4,64,512]{3,2,0,1:T(8,128)(2,1)S(1)} async-done(((bf16[3,4,64,512]{3,2,0,1:T(8,128)(2,1)}), bf16[3,4,64,512]{3,2,0,1:T(8,128)(2,1)S(1)}, u32[]{:S(2)}, u32[]{:S(2)}) %all-to-all-start) | async-done | bytes 786464 | tf_op jit(solution)/shard_map/all_to_all | solution.py:63
  41.1 1.3 collective-permute-start
  42.4 3.2 collective-permute-start.1
  46.8 2.2 fusion.123
  49.0 11.4 %fusion.7 = bf16[64,96,1024]{2,1,0:T(8,128)(2,1)S(1)} fusion(s32[64,96]{1,0:T(8,128)} %param.22, bf16[768,1024,1]{1,0,2:T(8,128)(2,1)S(1)} %fusion.123), kind=kOutput, calls=%fused_computation.12 | convolution fusion | flops 9674686464 | bytes 14180352 | tf_op jit(solution)/shard_map/gjc,ce->gje/dot_general | solution.py:77
  60.5 3.7 slice_bitcast_fusion.1
  64.3 3.3 fusion.14
  67.6 3.3 fusion.8
  71.2 3.6 fusion.39
  75.8 3.5 fusion.38
  81.0 5.0 %collective-permute-start.2 = (bf16[256,1024]{1,0:T(8,128)(2,1)S(1)}, bf16[256,1024]{1,0:T(8,128)(2,1)S(1)}, u32[]{:S(2)}, u32[]{:S(2)}) collective-permute-start(bf16[256,1024]{1,0:T(8,128)(2,1)S(1)} %get-tuple-element.20), channel_id=1, source_target_pairs={{0,4},{4,8},{8,12},{12,16},{16,20},{20,24},{24,28},{1,5},{5,9},{9,... | collective-permute-start | bytes 1572872 | tf_op jit(solution)/shard_map/ppermute | solution.py:13
  86.0 1.5 collective-permute-start.3
  87.5 4.2 %collective-permute-done.3 = bf16[256,1024]{1,0:T(8,128)(2,1)S(1)} collective-permute-done((bf16[256,1024]{1,0:T(8,128)(2,1)S(1)}, bf16[256,1024]{1,0:T(8,128)(2,1)S(1)}, u32[]{:S(2)}, u32[]{:S(2)}) %collective-permute-start.3) | collective-permute-done | bytes 524320 | tf_op jit(solution)/shard_map/ppermute | solution.py:13
  93.2 4.4 %all-to-all-start.1 = ((bf16[3,4,64,1024]{3,2,0,1:T(8,128)(2,1)}), bf16[3,4,64,1024]{3,2,0,1:T(8,128)(2,1)}, u32[]{:S(2)}, u32[]{:S(2)}) async-start(bf16[3,4,64,1024]{3,2,0,1:T(8,128)(2,1)} %copy.35), calls=%async_computation.1 | async-start | bytes 3145728 | tf_op jit(solution)/shard_map/all_to_all | solution.py:152
  97.7 4.7 %fusion.10 = f32[64,4,1,128]{3,2,1,0:T(1,128)S(1)} fusion(bf16[64,12,4,8,128]{4,3,2,1,0:T(8,128)(2,1)} %copy-done.2, bf16[64,4,96,1]{2,1,0,3:T(4,128)(2,1)S(1)} %copy-done.16), kind=kOutput, calls=%fused_computation.15 | convolution fusion | flops 6291456 | bytes 6471680 | tf_op jit(solution)/shard_map/gij,gjik->gik/dot_general | solution.py:96
  102.4 1.3 convolution_bitcast_fusion
  103.7 1.7 fusion.12
  105.9 25.0 %all-to-all-done.1 = bf16[3,4,64,1024]{3,2,0,1:T(8,128)(2,1)} async-done(((bf16[3,4,64,1024]{3,2,0,1:T(8,128)(2,1)}), bf16[3,4,64,1024]{3,2,0,1:T(8,128)(2,1)}, u32[]{:S(2)}, u32[]{:S(2)}) %all-to-all-start.1) | async-done | bytes 1572896 | tf_op jit(solution)/shard_map/all_to_all | solution.py:152
  130.8 1.6 copy.36
  134.2 2.5 pad_maximum_fusion
  137.7 166.7 %all-reduce.3.cloned.1.call-done = f32[4,512,512]{2,1,0:T(8,128)} async-done(((f32[4,512,512]{2,1,0:T(8,128)}), f32[4,512,512]{2,1,0:T(8,128)}) %all-reduce.3.cloned.1.call-update) | async-done | bytes 4194320 | tf_op jit(solution)/shard_map/psum | solution.py:181
  304.4 1.5 fusion.66
  306.8 2.7 fusion.93
  309.5 6.1 %fusion.28 = (f32[2048]{0:T(1024)S(1)}, f32[2048,512]{0,1:T(8,128)S(1)}) fusion(bf16[2048,512]{0,1:T(8,128)(2,1)S(1)} %copy-done.4, f32[512]{0:T(512)S(1)} %copy-done.27, f32[768,512]{1,0:T(8,128)S(1)} %fusion.93, s32[768]{0:T(1024)S(1)} %copy-done.25), kind=kOutput, calls=%fused_computation.36 | convolution fusion | flops 9669441536 | bytes 7877632 | tf_op jit(solution)/shard_map/sp,sd->pd/dot_general | solution.py:157
  315.6 2.5 fusion.27
  318.1 3.9 copy.37
  322.1 65.4 %all-reduce.5.cloned.1.call-done = f32[4,512,512]{2,1,0:T(8,128)} async-done(((f32[4,512,512]{2,1,0:T(8,128)}), f32[4,512,512]{2,1,0:T(8,128)}) %all-reduce.5.cloned.1.call-update) | async-done | bytes 4194320 | tf_op jit(solution)/shard_map/psum | solution.py:181
  387.5 4.6 %copy.107 = f32[4,512,512]{2,1,0:T(8,128)} copy(f32[4,512,512]{2,1,0:T(8,128)} %all-reduce.5.cloned.1.call-done) | data formatting | bytes 8388608
  (103 shorter events, 13.2 us)
Async XLA Ops:
  7.2 16.6 %copy-start = (bf16[512,512]{1,0:T(8,128)(2,1)S(1)}, bf16[512,512]{1,0:T(8,128)(2,1)}, u32[]{:S(2)}) copy-start(bf16[512,512]{1,0:T(8,128)(2,1)} %param.17) | copy-start | bytes 1572868
  7.2 3.5 copy-start.21
  7.2 3.6 copy-start.26
  10.8 10.2 %copy-start.6 = (bf16[64,512]{1,0:T(8,128)(2,1)S(1)}, bf16[64,512]{1,0:T(8,128)(2,1)}, u32[]{:S(2)}) copy-start(bf16[64,512]{1,0:T(8,128)(2,1)} %param.14) | copy-start | bytes 196612
  12.8 10.7 %copy-start.7 = (bf16[512,512]{1,0:T(8,128)(2,1)S(1)}, bf16[512,512]{1,0:T(8,128)(2,1)}, u32[]{:S(2)}) copy-start(bf16[512,512]{1,0:T(8,128)(2,1)} %param.20) | copy-start | bytes 1572868
  12.8 10.7 %copy-start.11 = (bf16[64,512]{1,0:T(8,128)(2,1)S(1)}, bf16[64,512]{1,0:T(8,128)(2,1)}, u32[]{:S(2)}) copy-start(bf16[64,512]{1,0:T(8,128)(2,1)} %param.25) | copy-start | bytes 196612
  13.7 10.1 %copy-start.18 = (f32[512]{0:T(512)S(1)}, f32[512]{0:T(512)}, u32[]{:S(2)}) copy-start(f32[512]{0:T(512)} %param.16) | copy-start | bytes 6148
  13.7 32.0 %copy-start.12 = (bf16[512,512]{1,0:T(8,128)(2,1)S(1)}, bf16[512,512]{1,0:T(8,128)(2,1)}, u32[]{:S(2)}) copy-start(bf16[512,512]{1,0:T(8,128)(2,1)} %param.19) | copy-start | bytes 1572868
  13.7 32.9 %copy-start.13 = (f32[64,384]{1,0:T(8,128)S(1)}, f32[64,384]{1,0:T(8,128)}, u32[]{:S(2)}) copy-start(f32[64,384]{1,0:T(8,128)} %param.21) | copy-start | bytes 294916
  13.7 33.1 %copy-start.17 = (s32[64,96]{1,0:T(8,128)S(1)}, s32[64,96]{1,0:T(8,128)}, u32[]{:S(2)}) copy-start(s32[64,96]{1,0:T(8,128)} %param.23) | copy-start | bytes 73732
  14.6 26.5 %all-to-all-start = ((bf16[3,4,64,512]{3,2,0,1:T(8,128)(2,1)}), bf16[3,4,64,512]{3,2,0,1:T(8,128)(2,1)S(1)}, u32[]{:S(2)}, u32[]{:S(2)}) async-start(bf16[3,4,64,512]{3,2,0,1:T(8,128)(2,1)} %copy.28), calls=%async_computation | async-start | bytes 1572864 | tf_op jit(solution)/shard_map/all_to_all | solution.py:63
  41.1 5.7 %collective-permute-start = (bf16[256,512]{1,0:T(8,128)(2,1)S(1)}, bf16[256,512]{1,0:T(8,128)(2,1)S(1)}, u32[]{:S(2)}, u32[]{:S(2)}) collective-permute-start(bf16[256,512]{1,0:T(8,128)(2,1)S(1)} %bitcast.120), channel_id=1, source_target_pairs={{4,0},{8,4},{12,8},{16,12},{20,16},{24,20},{28,24},{5,1},{9,5},{13... | collective-permute-start | bytes 786440 | tf_op jit(solution)/shard_map/ppermute | solution.py:13
  42.4 4.4 %collective-permute-start.1 = (bf16[256,512]{1,0:T(8,128)(2,1)S(1)}, bf16[256,512]{1,0:T(8,128)(2,1)S(1)}, u32[]{:S(2)}, u32[]{:S(2)}) collective-permute-start(bf16[256,512]{1,0:T(8,128)(2,1)S(1)} %bitcast.119), channel_id=1, source_target_pairs={{0,4},{4,8},{8,12},{12,16},{16,20},{20,24},{24,28},{1,5},{5,9},{9,... | collective-permute-start | bytes 786440 | tf_op jit(solution)/shard_map/ppermute | solution.py:13
  64.2 6.7 %copy-start.1 = (bf16[64,12,4,8,128]{4,3,2,1,0:T(8,128)(2,1)}, bf16[64,12,4,8,128]{4,3,2,1,0:T(8,128)(2,1)S(1)}, u32[]{:S(2)}) copy-start(bf16[64,12,4,8,128]{4,3,2,1,0:T(8,128)(2,1)S(1)} %get-tuple-element.16) | copy-start | bytes 18874372
  64.2 6.7 %copy-start.2 = (bf16[64,12,4,8,128]{4,3,2,1,0:T(8,128)(2,1)}, bf16[64,12,4,8,128]{4,3,2,1,0:T(8,128)(2,1)S(1)}, u32[]{:S(2)}) copy-start(bf16[64,12,4,8,128]{4,3,2,1,0:T(8,128)(2,1)S(1)} %get-tuple-element.17) | copy-start | bytes 18874372
  67.6 3.6 copy-start.28
  75.8 4.0 copy-start.14
  81.0 6.5 %collective-permute-start.2 = (bf16[256,1024]{1,0:T(8,128)(2,1)S(1)}, bf16[256,1024]{1,0:T(8,128)(2,1)S(1)}, u32[]{:S(2)}, u32[]{:S(2)}) collective-permute-start(bf16[256,1024]{1,0:T(8,128)(2,1)S(1)} %get-tuple-element.20), channel_id=1, source_target_pairs={{0,4},{4,8},{8,12},{12,16},{16,20},{20,24},{24,28},{1,5},{5,9},{9,... | collective-permute-start | bytes 1572872 | tf_op jit(solution)/shard_map/ppermute | solution.py:13
  86.0 5.8 %collective-permute-start.3 = (bf16[256,1024]{1,0:T(8,128)(2,1)S(1)}, bf16[256,1024]{1,0:T(8,128)(2,1)S(1)}, u32[]{:S(2)}, u32[]{:S(2)}) collective-permute-start(bf16[256,1024]{1,0:T(8,128)(2,1)S(1)} %get-tuple-element.21), channel_id=1, source_target_pairs={{4,0},{8,4},{12,8},{16,12},{20,16},{24,20},{28,24},{5,1},{9,5},{13... | collective-permute-start | bytes 1572872 | tf_op jit(solution)/shard_map/ppermute | solution.py:13
  91.7 5.9 %copy-start.16 = (bf16[64,4,96,1]{2,1,0,3:T(4,128)(2,1)S(1)}, bf16[64,4,96,1]{2,1,0,3:T(4,128)(2,1)}, u32[]{:S(2)}) copy-start(bf16[64,4,96,1]{2,1,0,3:T(4,128)(2,1)} %get-tuple-element.27) | copy-start | bytes 147460
  91.9 11.8 %slice-start = ((s8[6291456]{0:T(1024)(128)(4,1)}), s8[2097152]{0:T(1024)(128)(4,1)S(1)}, s32[]{:S(2)}) async-start(s8[6291456]{0:T(1024)(128)(4,1)} %bitcast.102), calls=%async_computation.4 | async-start | bytes 4194304
  93.2 37.6 %all-to-all-start.1 = ((bf16[3,4,64,1024]{3,2,0,1:T(8,128)(2,1)}), bf16[3,4,64,1024]{3,2,0,1:T(8,128)(2,1)}, u32[]{:S(2)}, u32[]{:S(2)}) async-start(bf16[3,4,64,1024]{3,2,0,1:T(8,128)(2,1)} %copy.35), calls=%async_computation.1 | async-start | bytes 3145728 | tf_op jit(solution)/shard_map/all_to_all | solution.py:152
  97.6 206.8 %all-reduce.3.cloned.1.call-start = ((), (), s32[]{:S(2)}) async-start(), calls=%async_computation.2 | async-start | bytes 8388608 | tf_op jit(solution)/shard_map/psum | solution.py:181
  97.7 6.0 %copy-start.15 = (bf16[64,4,96]{2,1,0:T(4,128)(2,1)S(1)}, bf16[64,4,96]{2,1,0:T(4,128)(2,1)}, u32[]{:S(2)}) copy-start(bf16[64,4,96]{2,1,0:T(4,128)(2,1)} %copy-done.14) | copy-start | bytes 147460
  97.7 6.0 %slice-start.1 = ((s8[6291456]{0:T(1024)(128)(4,1)}), s8[4194304]{0:T(1024)(128)(4,1)S(1)}, s32[]{:S(2)}) async-start(s8[6291456]{0:T(1024)(128)(4,1)} %bitcast.102), calls=%async_computation.5 | async-start | bytes 8388608
  102.3 3.1 copy-start.19
  102.3 3.1 copy-start.23
  105.4 27.0 %copy-start.10 = (bf16[768,512]{1,0:T(8,128)(2,1)S(1)}, bf16[768,512]{1,0:T(8,128)(2,1)}, u32[]{:S(2)}) copy-start(bf16[768,512]{1,0:T(8,128)(2,1)} %copy-done.9) | copy-start | bytes 2359300
  136.7 250.8 %all-reduce.5.cloned.1.call-start = ((), (), s32[]{:S(2)}) async-start(), calls=%async_computation.3 | async-start | bytes 8388608 | tf_op jit(solution)/shard_map/psum | solution.py:181
  304.4 5.1 %copy-start.4 = (bf16[2048,512]{0,1:T(8,128)(2,1)S(1)}, bf16[2048,512]{0,1:T(8,128)(2,1)}, u32[]{:S(2)}) copy-start(bf16[2048,512]{0,1:T(8,128)(2,1)} %copy-done.3) | copy-start | bytes 6291460
  304.4 5.1 %copy-start.25 = (s32[768]{0:T(1024)S(1)}, s32[768]{0:T(1024)}, u32[]{:S(2)}) copy-start(s32[768]{0:T(1024)} %copy-done.24) | copy-start | bytes 9220
  304.4 5.1 %copy-start.27 = (f32[512]{0:T(512)S(1)}, f32[512]{0:T(512)}, u32[]{:S(2)}) copy-start(f32[512]{0:T(512)} %param.15) | copy-start | bytes 6148
  (7 other events, 9.7 us)
Sparse Core Ops, SparseCore 0:
  136.8 167.5 all-reduce.2
  307.7 79.7 all-reduce.4
